TPU v7x, 32 devices: a whole 2x2x4 slice. The times are simulated.
32 devices in a mesh: grp: 2 (over x), tile: 16 (over z, y, core).
Axes of the slice: x: 2, y: 2, z: 4, core: 2. Of those that a mesh axis runs over, the one named last changes fastest.
Arguments:
- features: bfloat16 [384, 64, 2048], P('tile', 'grp'), may hold values from -6 to 6
- occupancy: int32 [192, 2, 16], P('tile', 'grp'), may hold values 0 or 1
- link_weights: int32 [4, 384, 64], P(None, 'tile', 'grp'), may hold values from 0 to 3
- basis_cols: bfloat16 [2048, 256], replicated, may hold values from -0.125 to 0.125
Outputs:
- product: float32 [2048, 256], P('tile')
All inputs are finite; a program needn't handle non-finite values. No bound on the sum of `occupancy` on one device may be relied on, other than what follows from the above.
Results may differ from a plain program's by a relative error of at most 0.004.
Values may be sent and summed in bfloat16 or wider, within the bound.
No kernel may reach another device: no remote copies, remote signals or barrier semaphores. Data moves between devices by JAX's collectives and lax.ppermute only.
A program may use at most 64 MiB of HBM per device.

v0:
```python
import math
import jax
import jax.numpy as jnp
from jax import lax
from jax.sharding import PartitionSpec as P


def extended(cells, sides, width):
    for axis, dim in sides:
        count = lax.axis_size(axis)
        ends = count - 1
        head = lax.slice_in_dim(cells, 0, width, axis=dim)
        tail = lax.slice_in_dim(cells, cells.shape[dim] - width, cells.shape[dim], axis=dim)
        cells = jnp.concatenate(
            [
                lax.ppermute(tail, axis, [(i, (i + 1) % count) for i in range(ends)]),
                cells,
                lax.ppermute(head, axis, [((i + 1) % count, i) for i in range(ends)]),
            ],
            axis=dim,
        )
    return cells


def apply_mask(feat_rows, mask_rows):
    lat_rows, lon_cols, word_count = feat_rows.shape
    groups = mask_rows.shape[1]
    word_blocks = mask_rows.shape[2]
    shaped = feat_rows.reshape(
        lat_rows // 2, 2, groups, lon_cols // groups, word_blocks, word_count // word_blocks
    )
    gate = mask_rows.astype(jnp.bfloat16)[:, None, :, None, :, None]
    return (shaped * gate).reshape(lat_rows * lon_cols, word_count)


def spatial_average(padded, link_weights):
    weights = link_weights.astype(jnp.float32)
    north_side = padded[:-2, 1:-1].astype(jnp.float32)
    south_side = padded[2:, 1:-1].astype(jnp.float32)
    west_side = padded[1:-1, :-2].astype(jnp.float32)
    east_side = padded[1:-1, 2:].astype(jnp.float32)
    weighted = weights[0][:, :, None] * north_side + weights[1][:, :, None] * south_side
    weighted = weighted + weights[2][:, :, None] * west_side + weights[3][:, :, None] * east_side
    weight_total = jnp.maximum(jnp.sum(weights, axis=0), 1.0)
    return (weighted / weight_total[:, :, None]).astype(jnp.bfloat16)


def per_device(features, occupancy, link_weights, basis_cols):
    lat_rows, lon_cols, word_count = features.shape
    rank_width = basis_cols.shape[1]
    masked = apply_mask(features, occupancy)
    projected = jnp.dot(masked, basis_cols, preferred_element_type=jnp.float32).astype(jnp.bfloat16)
    projected = projected.reshape(lat_rows, lon_cols, rank_width)
    padded = extended(projected, (("grp", 1), ("tile", 0)), 1)
    smooth = spatial_average(padded, link_weights).reshape(lat_rows * lon_cols, rank_width)
    scaling = 1.0 / math.sqrt(lat_rows * lon_cols * lax.axis_size("grp") * lax.axis_size("tile"))
    share_rows = word_count // lax.axis_size("tile")
    local_term = lax.dot_general(
        masked, smooth, (((0,), (0,)), ((), ())), preferred_element_type=jnp.float32
    )
    summed = lax.psum(local_term, ("grp", "tile"))
    own_rows = lax.dynamic_slice_in_dim(summed, lax.axis_index("tile") * share_rows, share_rows, 0)
    return own_rows * scaling


def solution(mesh):
    placed = (P("tile", "grp", None), P("tile", "grp", None), P(None, "tile", "grp"), P())
    return jax.shard_map(
        per_device, mesh=mesh, in_specs=placed, out_specs=P("tile", None), check_vma=False
    )
```

profile of v0, /device:TPU:0, one launch (start us, length us, event | category | flops | bytes accessed | tf_op | source)
XLA Modules:
  0.0 175.5 jit_solution(12780380878305803182)
XLA Ops:
  6.5 0.0 copy-start
  6.5 0.0 all-reduce.2.cloned.1.call-start
  6.5 0.0 copy-start.2
  6.5 0.8 convert_element_type.24
  7.4 0.5 mul.80
  7.9 0.0 copy-done
  7.9 0.9 copy-done.2
  8.8 0.0 copy-start.1
  8.8 1.0 fusion.8
  9.8 4.9 %collective-permute-start = (bf16[24,1,256]{2,1,0:T(2,128)(2,1)S(1)}, bf16[24,1,256]{2,1,0:T(2,128)(2,1)S(1)}, u32[]{:S(2)}, u32[]{:S(2)}) collective-permute-start(bf16[24,1,256]{2,1,0:T(2,128)(2,1)S(1)} %get-tuple-element.7), channel_id=1, source_target_pairs={{0,16},{1,17},{2,18},{3,19},{4,20},{5,21},{6,22},{7,23},{8,24},{9,... | collective-permute-start | bytes 36872 | tf_op jit(solution)/shard_map/ppermute | solution.py:16
  14.7 1.3 collective-permute-start.1
  16.0 0.0 copy-done.1
  16.1 0.1 collective-permute-done
  16.2 4.2 %collective-permute-done.1 = bf16[24,1,256]{2,1,0:T(2,128)(2,1)S(1)} collective-permute-done((bf16[24,1,256]{2,1,0:T(2,128)(2,1)S(1)}, bf16[24,1,256]{2,1,0:T(2,128)(2,1)S(1)}, u32[]{:S(2)}, u32[]{:S(2)}) %collective-permute-start.1) | collective-permute-done | bytes 12320 | tf_op jit(solution)/shard_map/ppermute | solution.py:18
  20.5 1.3 collective-permute-start.2
  21.8 1.3 collective-permute-start.3
  23.1 0.1 mul.74
  23.2 0.0 collective-permute-done.2
  23.2 3.4 %collective-permute-done.3 = bf16[1,34,256]{2,1,0:T(8,128)(2,1)S(1)} collective-permute-done((bf16[1,34,256]{2,1,0:T(8,128)(2,1)S(1)}, bf16[1,34,256]{2,1,0:T(8,128)(2,1)S(1)}, u32[]{:S(2)}, u32[]{:S(2)}) %collective-permute-start.3) | collective-permute-done | bytes 17440 | tf_op jit(solution)/shard_map/ppermute | solution.py:18
  26.6 3.2 %fusion.4 = f32[2048,256]{1,0:T(8,128)} fusion(bf16[24,32,2048]{2,1,0:T(8,128)(2,1)S(1)} %copy-done.2, bf16[24,2048]{1,0:T(8,128)(2,1)S(1)} %bitcast.34, bf16[24,1,256]{2,1,0:T(2,128)(2,1)S(1)} %collective-permute-done.1, bf16[24,32,256]{2,1,0:T(8,128)(2,1)S(1)} %bitcast.32, bf16[24,1,256]{2,1,0:T(2,128)(2,1)S(1)} %collective-permute-done, ...), kind=kOutput, calls=%fused_computation.5 | convolution fusion | flops 813367296 | bytes 5809152 | tf_op jit(solution)/shard_map/dot_general | solution.py:58
  29.8 0.0 all-reduce.2.cloned.1.call-update
  29.8 137.3 %all-reduce.2.cloned.1.call-done = f32[2048,256]{1,0:T(8,128)} async-done(((f32[2048,256]{1,0:T(8,128)}), f32[2048,256]{1,0:T(8,128)}) %all-reduce.2.cloned.1.call-update) | async-done | bytes 2097168 | tf_op jit(solution)/shard_map/psum | solution.py:61
  167.1 1.6 dynamic-slice_multiply_fusion
  (8 shorter events, 0.1 us)
Async XLA Ops:
  6.5 1.3 copy-start
  6.5 160.6 %all-reduce.2.cloned.1.call-start = ((), (), s32[]{:S(2)}) async-start(), calls=%async_computation | async-start | bytes 4194304 | tf_op jit(solution)/shard_map/psum | solution.py:61
  6.5 2.2 %copy-start.2 = (bf16[24,32,2048]{2,1,0:T(8,128)(2,1)S(1)}, bf16[24,32,2048]{2,1,0:T(8,128)(2,1)}, u32[]{:S(2)}) copy-start(bf16[24,32,2048]{2,1,0:T(8,128)(2,1)} %param.4) | copy-start | bytes 9437188
  8.8 7.3 %copy-start.1 = (s32[4,24,32]{2,1,0:T(8,128)S(1)}, s32[4,24,32]{2,1,0:T(8,128)}, u32[]{:S(2)}) copy-start(s32[4,24,32]{2,1,0:T(8,128)} %param.6) | copy-start | bytes 36868
  9.8 6.4 %collective-permute-start = (bf16[24,1,256]{2,1,0:T(2,128)(2,1)S(1)}, bf16[24,1,256]{2,1,0:T(2,128)(2,1)S(1)}, u32[]{:S(2)}, u32[]{:S(2)}) collective-permute-start(bf16[24,1,256]{2,1,0:T(2,128)(2,1)S(1)} %get-tuple-element.7), channel_id=1, source_target_pairs={{0,16},{1,17},{2,18},{3,19},{4,20},{5,21},{6,22},{7,23},{8,24},{9,... | collective-permute-start | bytes 36872 | tf_op jit(solution)/shard_map/ppermute | solution.py:16
  14.7 5.7 %collective-permute-start.1 = (bf16[24,1,256]{2,1,0:T(2,128)(2,1)S(1)}, bf16[24,1,256]{2,1,0:T(2,128)(2,1)S(1)}, u32[]{:S(2)}, u32[]{:S(2)}) collective-permute-start(bf16[24,1,256]{2,1,0:T(2,128)(2,1)S(1)} %get-tuple-element.8), channel_id=1, source_target_pairs={{16,0},{17,1},{18,2},{19,3},{20,4},{21,5},{22,6},{23,7},{24,8},{25... | collective-permute-start | bytes 36872 | tf_op jit(solution)/shard_map/ppermute | solution.py:18
  20.5 2.7 %collective-permute-start.2 = (bf16[1,34,256]{2,1,0:T(8,128)(2,1)S(1)}, bf16[1,34,256]{2,1,0:T(8,128)(2,1)S(1)}, u32[]{:S(2)}, u32[]{:S(2)}) collective-permute-start(bf16[1,34,256]{2,1,0:T(8,128)(2,1)S(1)} %get-tuple-element.5), channel_id=1, source_target_pairs={{0,1},{1,2},{2,3},{3,4},{4,5},{5,6},{6,7},{7,8},{8,9},{9,10},{10,1... | collective-permute-start | bytes 52232 | tf_op jit(solution)/shard_map/ppermute | solution.py:16
  21.8 4.8 %collective-permute-start.3 = (bf16[1,34,256]{2,1,0:T(8,128)(2,1)S(1)}, bf16[1,34,256]{2,1,0:T(8,128)(2,1)S(1)}, u32[]{:S(2)}, u32[]{:S(2)}) collective-permute-start(bf16[1,34,256]{2,1,0:T(8,128)(2,1)S(1)} %get-tuple-element.6), channel_id=1, source_target_pairs={{1,0},{2,1},{3,2},{4,3},{5,4},{6,5},{7,6},{8,7},{9,8},{10,9},{11,1... | collective-permute-start | bytes 52232 | tf_op jit(solution)/shard_map/ppermute | solution.py:18
Sparse Core Ops, SparseCore 0:
  29.9 137.1 all-reduce.1
where the time goes:
time: 176 us
  waiting for transfers between devices  145 us (82%)
  between operations  13.5 us (8%)
  starting transfers between devices  8.75 us (5%)
  matrix products  4.18 us (2%)
  other arithmetic  2.46 us (1%)
    psum x1, waiting for transfers between devices, per_device(): summed = lax.psum(local_term, ('grp', 'tile'))  137 us
    ppermute x2, waiting for transfers between devices, extended(): lax.ppermute(head, axis, [((i + 1) % count, i) for i in range(ends)])  7.61 us
    ppermute x2, starting transfers between devices, extended(): lax.ppermute(tail, axis, [(i, (i + 1) % count) for i in range(ends)])  6.16 us
  transfers between devices with their start and end apart: 5, of which 4 were waited for; matrix products, arithmetic and copies ran while one was open for 0% of the time, Pallas kernels for 0%

commit v1 on v0

--- a/solution.py
+++ b/solution.py
@@ -58,7 +58,7 @@
     local_term = lax.dot_general(
         masked, smooth, (((0,), (0,)), ((), ())), preferred_element_type=jnp.float32
     )
-    summed = lax.psum(local_term, ("grp", "tile"))
+    summed = lax.psum(lax.psum(local_term, "grp"), "tile")
     own_rows = lax.dynamic_slice_in_dim(summed, lax.axis_index("tile") * share_rows, share_rows, 0)
     return own_rows * scaling
 

time: 176 us -> 206 us (1.17)
  waiting for transfers between devices: 145 us -> 175 us
    psum x1 -> x2, waiting for transfers between devices: 137 us -> 167 us  [per_device(): summed = lax.psum(lax.psum(local_term, 'grp'), 'tile')]
  transfers between devices with their start and end apart: 5 -> 6, of which waited for: 4 -> 5; matrix products, arithmetic and copies ran while one was open for 0% -> 0% of each run, Pallas kernels for 0% -> 0%
where the time goes in v1:
time: 206 us; the launch traced here: 205 us
  waiting for transfers between devices  175 us (85%)
  between operations  13.5 us (7%)
  starting transfers between devices  8.79 us (4%)
  matrix products  4.18 us (2%)
  other arithmetic  2.46 us (1%)
    psum x2, waiting for transfers between devices, per_device(): summed = lax.psum(lax.psum(local_term, 'grp'), 'tile')  167 us
    ppermute x2, waiting for transfers between devices, extended(): lax.ppermute(head, axis, [((i + 1) % count, i) for i in range(ends)])  7.61 us
    ppermute x2, starting transfers between devices, extended(): lax.ppermute(tail, axis, [(i, (i + 1) % count) for i in range(ends)])  6.16 us
  transfers between devices with their start and end apart: 6, of which 5 were waited for; matrix products, arithmetic and copies ran while one was open for 0% of the time, Pallas kernels for 0%

profile of v1, /device:TPU:0, one launch (start us, length us, event | category | flops | bytes accessed | tf_op | source)
XLA Modules:
  0.0 205.5 jit_solution(9749530647385877107)
XLA Ops:
  6.5 0.0 copy-start
  6.5 0.0 all-reduce.3.cloned.1.call-start
  6.5 0.0 copy-start.2
  6.5 0.8 convert_element_type.24
  7.4 0.5 mul.80
  7.9 0.0 copy-done
  7.9 0.9 copy-done.2
  8.8 0.0 copy-start.1
  8.8 1.0 fusion.8
  9.8 4.9 %collective-permute-start = (bf16[24,1,256]{2,1,0:T(2,128)(2,1)S(1)}, bf16[24,1,256]{2,1,0:T(2,128)(2,1)S(1)}, u32[]{:S(2)}, u32[]{:S(2)}) collective-permute-start(bf16[24,1,256]{2,1,0:T(2,128)(2,1)S(1)} %get-tuple-element.7), channel_id=1, source_target_pairs={{0,16},{1,17},{2,18},{3,19},{4,20},{5,21},{6,22},{7,23},{8,24},{9,... | collective-permute-start | bytes 36872 | tf_op jit(solution)/shard_map/ppermute | solution.py:16
  14.7 1.3 collective-permute-start.1
  16.0 0.0 copy-done.1
  16.1 0.1 collective-permute-done
  16.2 4.2 %collective-permute-done.1 = bf16[24,1,256]{2,1,0:T(2,128)(2,1)S(1)} collective-permute-done((bf16[24,1,256]{2,1,0:T(2,128)(2,1)S(1)}, bf16[24,1,256]{2,1,0:T(2,128)(2,1)S(1)}, u32[]{:S(2)}, u32[]{:S(2)}) %collective-permute-start.1) | collective-permute-done | bytes 12320 | tf_op jit(solution)/shard_map/ppermute | solution.py:18
  20.5 1.3 collective-permute-start.2
  21.8 1.3 collective-permute-start.3
  23.1 0.1 mul.74
  23.2 0.0 collective-permute-done.2
  23.2 3.4 %collective-permute-done.3 = bf16[1,34,256]{2,1,0:T(8,128)(2,1)S(1)} collective-permute-done((bf16[1,34,256]{2,1,0:T(8,128)(2,1)S(1)}, bf16[1,34,256]{2,1,0:T(8,128)(2,1)S(1)}, u32[]{:S(2)}, u32[]{:S(2)}) %collective-permute-start.3) | collective-permute-done | bytes 17440 | tf_op jit(solution)/shard_map/ppermute | solution.py:18
  26.6 3.2 %fusion.4 = f32[2048,256]{1,0:T(8,128)} fusion(bf16[24,32,2048]{2,1,0:T(8,128)(2,1)S(1)} %copy-done.2, bf16[24,2048]{1,0:T(8,128)(2,1)S(1)} %bitcast.34, bf16[24,1,256]{2,1,0:T(2,128)(2,1)S(1)} %collective-permute-done.1, bf16[24,32,256]{2,1,0:T(8,128)(2,1)S(1)} %bitcast.32, bf16[24,1,256]{2,1,0:T(2,128)(2,1)S(1)} %collective-permute-done, ...), kind=kOutput, calls=%fused_computation.5 | convolution fusion | flops 813367296 | bytes 5809152 | tf_op jit(solution)/shard_map/dot_general | solution.py:58
  29.8 0.0 all-reduce.3.cloned.1.call-update
  29.8 0.0 all-reduce.5.cloned.1.call-start
  29.8 65.4 %all-reduce.3.cloned.1.call-done = f32[2048,256]{1,0:T(8,128)} async-done(((f32[2048,256]{1,0:T(8,128)}), f32[2048,256]{1,0:T(8,128)}) %all-reduce.3.cloned.1.call-update) | async-done | bytes 2097168 | tf_op jit(solution)/shard_map/psum | solution.py:61
  95.3 0.0 all-reduce.5.cloned.1.call-update
  95.3 101.7 %all-reduce.5.cloned.1.call-done = f32[2048,256]{1,0:T(8,128)} async-done(((f32[2048,256]{1,0:T(8,128)}), f32[2048,256]{1,0:T(8,128)}) %all-reduce.5.cloned.1.call-update) | async-done | bytes 2097168 | tf_op jit(solution)/shard_map/psum | solution.py:61
  197.0 1.6 dynamic-slice_multiply_fusion
  (8 shorter events, 0.1 us)
Async XLA Ops:
  6.5 1.3 copy-start
  6.5 88.7 %all-reduce.3.cloned.1.call-start = ((), (), s32[]{:S(2)}) async-start(), calls=%async_computation | async-start | bytes 4194304 | tf_op jit(solution)/shard_map/psum | solution.py:61
  6.5 2.2 %copy-start.2 = (bf16[24,32,2048]{2,1,0:T(8,128)(2,1)S(1)}, bf16[24,32,2048]{2,1,0:T(8,128)(2,1)}, u32[]{:S(2)}) copy-start(bf16[24,32,2048]{2,1,0:T(8,128)(2,1)} %param.4) | copy-start | bytes 9437188
  8.8 7.3 %copy-start.1 = (s32[4,24,32]{2,1,0:T(8,128)S(1)}, s32[4,24,32]{2,1,0:T(8,128)}, u32[]{:S(2)}) copy-start(s32[4,24,32]{2,1,0:T(8,128)} %param.6) | copy-start | bytes 36868
  9.8 6.4 %collective-permute-start = (bf16[24,1,256]{2,1,0:T(2,128)(2,1)S(1)}, bf16[24,1,256]{2,1,0:T(2,128)(2,1)S(1)}, u32[]{:S(2)}, u32[]{:S(2)}) collective-permute-start(bf16[24,1,256]{2,1,0:T(2,128)(2,1)S(1)} %get-tuple-element.7), channel_id=1, source_target_pairs={{0,16},{1,17},{2,18},{3,19},{4,20},{5,21},{6,22},{7,23},{8,24},{9,... | collective-permute-start | bytes 36872 | tf_op jit(solution)/shard_map/ppermute | solution.py:16
  14.7 5.7 %collective-permute-start.1 = (bf16[24,1,256]{2,1,0:T(2,128)(2,1)S(1)}, bf16[24,1,256]{2,1,0:T(2,128)(2,1)S(1)}, u32[]{:S(2)}, u32[]{:S(2)}) collective-permute-start(bf16[24,1,256]{2,1,0:T(2,128)(2,1)S(1)} %get-tuple-element.8), channel_id=1, source_target_pairs={{16,0},{17,1},{18,2},{19,3},{20,4},{21,5},{22,6},{23,7},{24,8},{25... | collective-permute-start | bytes 36872 | tf_op jit(solution)/shard_map/ppermute | solution.py:18
  20.5 2.7 %collective-permute-start.2 = (bf16[1,34,256]{2,1,0:T(8,128)(2,1)S(1)}, bf16[1,34,256]{2,1,0:T(8,128)(2,1)S(1)}, u32[]{:S(2)}, u32[]{:S(2)}) collective-permute-start(bf16[1,34,256]{2,1,0:T(8,128)(2,1)S(1)} %get-tuple-element.5), channel_id=1, source_target_pairs={{0,1},{1,2},{2,3},{3,4},{4,5},{5,6},{6,7},{7,8},{8,9},{9,10},{10,1... | collective-permute-start | bytes 52232 | tf_op jit(solution)/shard_map/ppermute | solution.py:16
  21.8 4.8 %collective-permute-start.3 = (bf16[1,34,256]{2,1,0:T(8,128)(2,1)S(1)}, bf16[1,34,256]{2,1,0:T(8,128)(2,1)S(1)}, u32[]{:S(2)}, u32[]{:S(2)}) collective-permute-start(bf16[1,34,256]{2,1,0:T(8,128)(2,1)S(1)} %get-tuple-element.6), channel_id=1, source_target_pairs={{1,0},{2,1},{3,2},{4,3},{5,4},{6,5},{7,6},{8,7},{9,8},{10,9},{11,1... | collective-permute-start | bytes 52232 | tf_op jit(solution)/shard_map/ppermute | solution.py:18
  29.8 167.3 %all-reduce.5.cloned.1.call-start = ((), (), s32[]{:S(2)}) async-start(), calls=%async_computation.1 | async-start | bytes 4194304 | tf_op jit(solution)/shard_map/psum | solution.py:61
Sparse Core Ops, SparseCore 0:
  29.9 65.3 all-reduce.2
  98.8 98.1 all-reduce.4
